TPU v7x, 32 devices: a whole 2x2x4 slice. The times are simulated.
32 devices in a mesh: seq: 8 (over y, x, core), batch: 4 (over z).
Axes of the slice: x: 2, y: 2, z: 4, core: 2. Of those that a mesh axis runs over, the one named last changes fastest.
Arguments:
- tokens: bfloat16 [4, 4096, 2048], P('batch', 'seq'), may hold values from -6 to 6
- w_qkv: bfloat16 [2048, 3072], replicated, may hold values from -0.125 to 0.125
- cotangent: bfloat16 [4, 4096, 1024], P('batch', 'seq'), may hold values from -6 to 6
Outputs:
- attended: bfloat16 [4, 4096, 1024], P('batch', 'seq')
- token_grad: bfloat16 [4, 4096, 2048], P('batch', 'seq')
- weight_grad: float32 [2048, 3072], P('seq')
All inputs are finite; a program needn't handle non-finite values.
Results may differ from a plain program's by a relative error of at most 0.0064.
Values sent between devices are 32-bit elements; how exact they have to be, the bound alone decides.
A program may use at most 192 MiB of HBM per device.

v0:
```python
import jax
import jax.numpy as jnp
from jax import lax
from jax.sharding import PartitionSpec as P

HEADS = 8
DH = 128
BLK = 512
PRECISE = lax.Precision.HIGHEST


def running_states(block_states, incoming, reverse):
    zero_block = jnp.zeros_like(block_states)
    if reverse:
        totals = jnp.cumsum(block_states[::-1], axis=0)[::-1]
        return incoming[None] + jnp.concatenate([totals[1:], zero_block], 0)
    totals = jnp.cumsum(block_states, axis=0)
    return incoming[None] + jnp.concatenate([zero_block, totals[:-1]], 0)


def body(tokens, w_qkv, cotangent):
    row_count = tokens.shape[1]
    width = w_qkv.shape[1] // 3
    block_count = row_count // BLK
    seq_count = lax.axis_size("seq")
    batch_count = lax.axis_size("batch")
    local_x = tokens[0]
    projected = jnp.dot(local_x, w_qkv, preferred_element_type=jnp.float32).astype(jnp.bfloat16)
    queries = projected[:, :width].reshape(block_count, BLK, HEADS, DH)
    key_heads = projected[:, width : 2 * width].reshape(block_count, BLK, HEADS, DH)
    value_heads = projected[:, 2 * width :].reshape(block_count, BLK, HEADS, DH)
    position = lax.axis_index("seq") * row_count + jnp.arange(row_count, dtype=jnp.int32)
    pos_scale = DH ** (-0.5) / jnp.sqrt(position.astype(jnp.float32) + 1.0)
    scaled_grad = (cotangent[0].astype(jnp.float32) * pos_scale[:, None]).astype(jnp.bfloat16)
    grad_heads = scaled_grad.reshape(block_count, BLK, HEADS, DH)
    kv_blocks = jnp.einsum(
        "nrha,nrhb->nhab", key_heads, value_heads, preferred_element_type=jnp.float32
    )
    grad_blocks = jnp.einsum(
        "nrha,nrhb->nhab", queries, grad_heads, preferred_element_type=jnp.float32
    )
    kv_local = jnp.sum(kv_blocks, 0)
    grad_local = jnp.sum(grad_blocks, 0)
    kv_all, grad_all = (
        lax.all_gather(kv_local[None], "seq", axis=0, tiled=True),
        lax.all_gather(grad_local[None], "seq", axis=0, tiled=True),
    )
    rank_list = jnp.arange(seq_count, dtype=jnp.int32)
    my_rank = lax.axis_index("seq")
    kv_in = jnp.sum(jnp.where((rank_list < my_rank)[:, None, None, None], kv_all, 0.0), 0)
    grad_in = jnp.sum(jnp.where((rank_list > my_rank)[:, None, None, None], grad_all, 0.0), 0)
    kv_before = running_states(kv_blocks, kv_in, False)
    grad_after = running_states(grad_blocks, grad_in, True)
    causal = jnp.arange(BLK)[:, None] >= jnp.arange(BLK)[None, :]
    scores = jnp.where(
        causal,
        jnp.einsum("nihd,njhd->nhij", queries, key_heads, preferred_element_type=jnp.float32),
        0.0,
    ).astype(jnp.bfloat16)
    grad_scores = jnp.where(
        causal,
        jnp.einsum("nihd,njhd->nhij", grad_heads, value_heads, preferred_element_type=jnp.float32),
        0.0,
    ).astype(jnp.bfloat16)
    query_wide = queries.astype(jnp.float32)
    key_wide = key_heads.astype(jnp.float32)
    value_wide = value_heads.astype(jnp.float32)
    grad_wide = grad_heads.astype(jnp.float32)
    attended = jnp.einsum(
        "nhij,njhd->nihd", scores, value_heads, preferred_element_type=jnp.float32
    )
    attended = attended + jnp.einsum("nihd,nhde->nihe", query_wide, kv_before, precision=PRECISE)
    attended = attended * pos_scale.reshape(block_count, BLK, 1, 1)
    query_grad = jnp.einsum(
        "nhij,njhd->nihd", grad_scores, key_heads, preferred_element_type=jnp.float32
    )
    query_grad = query_grad + jnp.einsum("nihe,nhde->nihd", grad_wide, kv_before, precision=PRECISE)
    key_grad = jnp.einsum(
        "nhij,nihd->njhd", grad_scores, queries, preferred_element_type=jnp.float32
    )
    key_grad = key_grad + jnp.einsum("njhe,nhde->njhd", value_wide, grad_after, precision=PRECISE)
    value_grad = jnp.einsum(
        "nhij,nihe->njhe", scores, grad_heads, preferred_element_type=jnp.float32
    )
    value_grad = value_grad + jnp.einsum("njhd,nhde->njhe", key_wide, grad_after, precision=PRECISE)
    qkv_grad = jnp.concatenate(
        [
            query_grad.reshape(row_count, width),
            key_grad.reshape(row_count, width),
            value_grad.reshape(row_count, width),
        ],
        1,
    ).astype(jnp.bfloat16)
    token_grad = lax.dot_general(
        qkv_grad, w_qkv, (((1,), (1,)), ((), ())), preferred_element_type=jnp.float32
    )
    token_grad = token_grad.astype(jnp.bfloat16)[None]
    partial_rows = lax.psum_scatter(
        lax.dot_general(
            local_x, qkv_grad, (((0,), (0,)), ((), ())), preferred_element_type=jnp.float32
        ),
        "seq",
        scatter_dimension=0,
        tiled=True,
    )
    summed = lax.psum(partial_rows, "batch")
    grad_scale = 1.0 / jnp.sqrt(jnp.float32(batch_count * seq_count * row_count))
    weight_grad = summed * grad_scale
    return (attended.reshape(row_count, width).astype(jnp.bfloat16)[None], token_grad, weight_grad)


def solution(mesh):
    return jax.shard_map(
        body,
        mesh=mesh,
        in_specs=(P("batch", "seq", None), P(), P("batch", "seq", None)),
        out_specs=(P("batch", "seq", None), P("batch", "seq", None), P("seq", None)),
        check_vma=False,
    )
```

profile of v0, /device:TPU:0, one launch (start us, length us, event | category | flops | bytes accessed | tf_op | source)
XLA Modules:
  0.0 420.3 jit_solution(13077857208843234971)
XLA Ops:
  7.2 0.0 copy-start
  7.2 0.0 all-gather.7.cloned.1.call-start
  7.2 2.7 copy.51
  10.0 9.6 %convolution_convert_fusion = bf16[512,3072]{1,0:T(8,128)(2,1)S(1)} fusion(bf16[2048,3072]{1,0:T(8,128)(2,1)} %param.4, bf16[1,512,2048]{2,1,0:T(8,128)(2,1)S(1)} %copy-done), kind=kOutput, calls=%fused_computation.3 | convolution fusion | flops 6444023808 | bytes 17825792 | tf_op jit(solution)/shard_map/dot_general | solution.py:28
  19.6 2.2 slice_bitcast_fusion.2
  21.8 2.3 copy.52
  24.1 2.0 multiply_convert_fusion
  26.0 1.0 copy-done.6
  27.1 1.2 fusion.22
  28.3 0.0 all-gather.7.cloned.1.call-update
  28.3 0.0 all-gather.5.cloned.1.call-start
  28.4 2.5 copy.55
  30.9 2.4 copy.29
  33.3 2.5 fusion.10
  35.7 0.0 all-gather.5.cloned.1.call-update
  35.8 0.2 reduce-scatter.2.cloned.1.call-start
  36.0 0.1 iota_compare_fusion
  36.1 2.8 select_convert_fusion
  38.9 1.5 select_convert_fusion.1
  40.4 0.0 copy-start.9
  40.4 2.0 fusion.21
  42.5 2.9 fusion.20
  45.4 0.0 copy-done.2
  45.4 2.0 fusion.23
  47.4 20.4 %all-gather.7.cloned.1.call-done = f32[64,128,128]{2,1,0:T(8,128)} async-done(((f32[8,128,128]{2,1,0:T(8,128)}), f32[64,128,128]{2,1,0:T(8,128)}) %all-gather.7.cloned.1.call-update) | async-done | bytes 4194320 | tf_op jit(solution)/shard_map/all_gather | solution.py:46
  67.8 2.9 select_reduce_fusion
  70.7 0.2 copy-done.16
  70.9 2.2 add_convert_fusion
  73.1 0.0 copy-done.11
  73.1 2.1 add_convert_fusion.1
  75.2 31.1 %all-gather.5.cloned.1.call-done = f32[64,128,128]{2,1,0:T(8,128)} async-done(((f32[8,128,128]{2,1,0:T(8,128)}), f32[64,128,128]{2,1,0:T(8,128)}) %all-gather.5.cloned.1.call-update) | async-done | bytes 4194320 | tf_op jit(solution)/shard_map/all_gather | solution.py:45
  106.3 2.9 select_reduce_fusion.1
  109.2 0.3 copy-done.10
  109.5 1.1 add_convert_fusion.2
  110.7 1.0 copy-done.19
  111.6 15.2 %convolution_bitcast_fusion = f32[2048,3072]{0,1:T(8,128)} fusion(bf16[1,512,2048]{2,1,0:T(8,128)(2,1)S(1)} %copy-done, bf16[512,1024]{0,1:T(8,128)(2,1)S(1)} %bitcast.86, bf16[512,1024]{0,1:T(8,128)(2,1)S(1)} %bitcast.88, bf16[512,1024]{0,1:T(8,128)(2,1)S(1)} %bitcast.89), kind=kOutput, calls=%fused_computation | convolution fusion | flops 6451888128 | bytes 30408704 | tf_op jit(solution)/shard_map/dot_general | solution.py:99
  126.8 0.0 reduce-scatter.2.cloned.1.call-update
  126.8 0.0 all-reduce.2.cloned.1.call-start
  126.9 156.1 %reduce-scatter.2.cloned.1.call-done = f32[256,3072]{0,1:T(8,128)} async-done(((f32[2048,3072]{0,1:T(8,128)}), f32[256,3072]{0,1:T(8,128)}) %reduce-scatter.2.cloned.1.call-update) | async-done | bytes 3145744 | tf_op jit(solution)/shard_map/reduce_scatter | solution.py:98
  283.0 0.0 all-reduce.2.cloned.1.call-update
  283.0 0.0 copy-start.14
  283.0 3.8 fusion.6
  286.9 1.1 fusion.1
  288.0 1.3 copy.44
  289.3 13.6 %fusion = bf16[1,512,2048]{2,1,0:T(8,128)(2,1)} fusion(bf16[2048,3072]{1,0:T(8,128)(2,1)} %param.4, bf16[512,1024]{0,1:T(8,128)(2,1)} %bitcast.85, bf16[512,1024]{0,1:T(8,128)(2,1)} %bitcast.87, bf16[512,1024]{0,1:T(8,128)(2,1)} %bitcast.90), kind=kOutput, calls=%fused_computation.8 | convolution fusion | flops 6452936704 | bytes 17825792 | tf_op jit(solution)/shard_map/dot_general | solution.py:94
  302.9 103.4 %all-reduce.2.cloned.1.call-done = f32[256,3072]{0,1:T(8,128)} async-done(((f32[256,3072]{0,1:T(8,128)}), f32[256,3072]{0,1:T(8,128)}) %all-reduce.2.cloned.1.call-update) | async-done | bytes 3145744 | tf_op jit(solution)/shard_map/psum | solution.py:106
  406.3 3.9 broadcast_multiply_fusion
  410.2 3.5 copy.45
  (34 shorter events, 0.1 us)
Async XLA Ops:
  7.2 2.8 copy-start
  7.2 60.6 %all-gather.7.cloned.1.call-start = ((), (), s32[]{:S(2)}) async-start(), calls=%async_computation.4 | async-start | bytes 4718592 | tf_op jit(solution)/shard_map/all_gather | solution.py:46
  24.1 3.0 copy-start.3
  26.0 1.0 copy-start.6
  28.3 78.0 %all-gather.5.cloned.1.call-start = ((), (), s32[]{:S(2)}) async-start(), calls=%async_computation.3 | async-start | bytes 4718592 | tf_op jit(solution)/shard_map/all_gather | solution.py:45
  35.8 247.2 %reduce-scatter.2.cloned.1.call-start = ((), (), s32[]{:S(2)}) async-start(), calls=%async_computation.1 | async-start | bytes 28311552 | tf_op jit(solution)/shard_map/reduce_scatter | solution.py:98
  36.1 2.8 copy-start.4
  36.1 2.8 copy-start.15
  40.4 4.9 %copy-start.2 = (bf16[8,512,512]{2,1,0:T(8,128)(2,1)}, bf16[8,512,512]{2,1,0:T(8,128)(2,1)S(1)}, u32[]{:S(2)}) copy-start(bf16[8,512,512]{2,1,0:T(8,128)(2,1)S(1)} %select_convert_fusion.1) | copy-start | bytes 12582916
  40.4 2.0 copy-start.9
  42.5 2.9 copy-start.7
  67.8 2.9 copy-start.12
  67.8 3.1 copy-start.16
  70.9 2.2 copy-start.11
  106.3 2.9 copy-start.8
  106.3 3.2 copy-start.10
  109.5 1.2 copy-start.13
  109.5 2.1 copy-start.17
  109.5 2.1 copy-start.18
  110.7 1.0 copy-start.19
  126.8 279.5 %all-reduce.2.cloned.1.call-start = ((), (), s32[]{:S(2)}) async-start(), calls=%async_computation.2 | async-start | bytes 6291456 | tf_op jit(solution)/shard_map/psum | solution.py:106
  283.0 3.8 copy-start.5
  283.0 3.8 copy-start.14
  406.3 7.5 %copy-start.1 = (bf16[1,512,2048]{2,1,0:T(8,128)(2,1)S(1)}, bf16[1,512,2048]{2,1,0:T(8,128)(2,1)}, u32[]{:S(2)}) copy-start(bf16[1,512,2048]{2,1,0:T(8,128)(2,1)} %param.3) | copy-start | bytes 6291460
Sparse Core Ops, SparseCore 0:
  28.5 39.3 all-gather.6
  69.7 36.5 all-gather.4
  126.9 156.0 reduce-scatter.1
  285.2 121.0 all-reduce.1
where the time goes:
time: 421 us; the launch traced here: 420 us
  waiting for transfers between devices  311 us (74%)
  matrix products  63.7 us (15%)
  local copies, waits for them, and re-layouts  19.4 us (5%)
  between operations  14 us (3%)
  other arithmetic  11.8 us (3%)
    reduce_scatter x1, waiting for transfers between devices, body(): lax.psum_scatter(lax.dot_general(local_x, qkv_grad, (((0,), (0,)), ((), (...  156 us
    psum x1, waiting for transfers between devices, body(): summed = lax.psum(partial_rows, 'batch')  103 us
    all_gather x1, waiting for transfers between devices, body(): lax.all_gather(kv_local[None], 'seq', axis=0, tiled=True)  31.1 us
    all_gather x1, waiting for transfers between devices, body(): lax.all_gather(grad_local[None], 'seq', axis=0, tiled=True)  20.4 us
    dot_general x1, matrix products, body(): lax.dot_general(local_x, qkv_grad, (((0,), (0,)), ((), ())), preferred_el...  15.2 us
    dot_general x1, matrix products, body(): lax.dot_general(qkv_grad, w_qkv, (((1,), (1,)), ((), ())), preferred_elem...  13.6 us
    unnamed x44, local copies, waits for them, and re-layouts  12 us
    dot_general x1, matrix products, body(): jnp.dot(local_x, w_qkv, preferred_element_type=jnp.float32)  9.63 us
  transfers between devices with their start and end apart: 4, of which 4 were waited for; matrix products, arithmetic and copies ran while one was open for 11% of the time, Pallas kernels for 0%

commit v1 on v0

--- a/solution.py
+++ b/solution.py
@@ -103,7 +103,8 @@
         scatter_dimension=0,
         tiled=True,
     )
-    summed = lax.psum(partial_rows, "batch")
+    terms = lax.all_gather(partial_rows, "batch")
+    summed = jnp.sum(terms, axis=0)
     grad_scale = 1.0 / jnp.sqrt(jnp.float32(batch_count * seq_count * row_count))
     weight_grad = summed * grad_scale
     return (attended.reshape(row_count, width).astype(jnp.bfloat16)[None], token_grad, weight_grad)

time: 421 us -> 552 us (1.31)
  waiting for transfers between devices: 311 us -> 406 us
  other arithmetic: 11.8 us -> 31.3 us
  local copies, waits for them, and re-layouts: 19.4 us -> 35.2 us
    all_gather x0 -> x1, waiting for transfers between devices: none -> 198 us  [body(): terms = lax.all_gather(partial_rows, 'batch')]
    psum x1 -> x0, waiting for transfers between devices: 103 us -> none  [body(): summed = lax.psum(partial_rows, 'batch')]
    reduce_sum x0 -> x1, other arithmetic: none -> 19.5 us  [body(): summed = jnp.sum(terms, axis=0)]
    all_gather x0 -> x1, local copies, waits for them, and re-layouts: none -> 15.5 us  [body(): terms = lax.all_gather(partial_rows, 'batch')]
  transfers between devices with their start and end apart: 4 -> 4, of which waited for: 4 -> 4; matrix products, arithmetic and copies ran while one was open for 11% -> 9% of each run, Pallas kernels for 0% -> 0%
where the time goes in v1:
time: 552 us
  waiting for transfers between devices  406 us (74%)
  matrix products  65 us (12%)
  local copies, waits for them, and re-layouts  35.2 us (6%)
  other arithmetic  31.3 us (6%)
  between operations  14 us (3%)
    all_gather x1, waiting for transfers between devices, body(): terms = lax.all_gather(partial_rows, 'batch')  198 us
    reduce_scatter x1, waiting for transfers between devices, body(): lax.psum_scatter(lax.dot_general(local_x, qkv_grad, (((0,), (0,)), ((), (...  156 us
    all_gather x1, waiting for transfers between devices, body(): lax.all_gather(kv_local[None], 'seq', axis=0, tiled=True)  31.1 us
    all_gather x1, waiting for transfers between devices, body(): lax.all_gather(grad_local[None], 'seq', axis=0, tiled=True)  20.4 us
    reduce_sum x1, other arithmetic, body(): summed = jnp.sum(terms, axis=0)  19.5 us
    all_gather x1, local copies, waits for them, and re-layouts, body(): terms = lax.all_gather(partial_rows, 'batch')  15.5 us
    dot_general x1, matrix products, body(): lax.dot_general(local_x, qkv_grad, (((0,), (0,)), ((), ())), preferred_el...  15.2 us
    dot_general x1, matrix products, body(): lax.dot_general(qkv_grad, w_qkv, (((1,), (1,)), ((), ())), preferred_elem...  14.9 us
  transfers between devices with their start and end apart: 4, of which 4 were waited for; matrix products, arithmetic and copies ran while one was open for 9% of the time, Pallas kernels for 0%

profile of v1, /device:TPU:0, one launch (start us, length us, event | category | flops | bytes accessed | tf_op | source)
XLA Modules:
  0.0 551.6 jit_solution(14196115651064449253)
XLA Ops:
  7.2 0.0 copy-start
  7.2 0.0 all-gather.9.cloned.1.call-start
  7.2 2.7 copy.50
  10.0 9.6 %convolution_convert_fusion = bf16[512,3072]{1,0:T(8,128)(2,1)S(1)} fusion(bf16[2048,3072]{1,0:T(8,128)(2,1)} %param.4, bf16[1,512,2048]{2,1,0:T(8,128)(2,1)S(1)} %copy-done), kind=kOutput, calls=%fused_computation.3 | convolution fusion | flops 6444023808 | bytes 17825792 | tf_op jit(solution)/shard_map/dot_general | solution.py:28
  19.6 2.2 slice_bitcast_fusion.2
  21.8 2.3 copy.51
  24.1 2.0 multiply_convert_fusion
  26.0 1.0 copy-done.6
  27.1 1.2 fusion.22
  28.3 0.0 all-gather.9.cloned.1.call-update
  28.3 0.0 all-gather.7.cloned.1.call-start
  28.4 2.5 copy.54
  30.9 2.4 copy.28
  33.3 2.5 fusion.10
  35.7 0.0 all-gather.7.cloned.1.call-update
  35.8 0.2 reduce-scatter.2.cloned.1.call-start
  36.0 0.1 iota_compare_fusion
  36.1 2.8 select_convert_fusion
  38.9 1.5 select_convert_fusion.1
  40.4 0.0 copy-start.9
  40.4 2.0 fusion.21
  42.5 2.9 fusion.20
  45.4 2.0 fusion.23
  47.4 20.4 %all-gather.9.cloned.1.call-done = f32[64,128,128]{2,1,0:T(8,128)} async-done(((f32[8,128,128]{2,1,0:T(8,128)}), f32[64,128,128]{2,1,0:T(8,128)}) %all-gather.9.cloned.1.call-update) | async-done | bytes 4194320 | tf_op jit(solution)/shard_map/all_gather | solution.py:46
  67.8 2.9 select_reduce_fusion
  70.7 0.2 copy-done.16
  70.9 2.2 add_convert_fusion
  73.1 2.1 add_convert_fusion.1
  75.2 31.1 %all-gather.7.cloned.1.call-done = f32[64,128,128]{2,1,0:T(8,128)} async-done(((f32[8,128,128]{2,1,0:T(8,128)}), f32[64,128,128]{2,1,0:T(8,128)}) %all-gather.7.cloned.1.call-update) | async-done | bytes 4194320 | tf_op jit(solution)/shard_map/all_gather | solution.py:45
  106.3 2.9 select_reduce_fusion.1
  109.2 0.3 copy-done.10
  109.5 1.1 add_convert_fusion.2
  110.7 1.0 copy-done.19
  111.6 15.2 %convolution_bitcast_fusion = f32[2048,3072]{0,1:T(8,128)} fusion(bf16[1,512,2048]{2,1,0:T(8,128)(2,1)S(1)} %copy-done, bf16[512,1024]{0,1:T(8,128)(2,1)S(1)} %bitcast.88, bf16[512,1024]{0,1:T(8,128)(2,1)S(1)} %bitcast.90, bf16[512,1024]{0,1:T(8,128)(2,1)S(1)} %bitcast.91), kind=kOutput, calls=%fused_computation | convolution fusion | flops 6451888128 | bytes 30408704 | tf_op jit(solution)/shard_map/dot_general | solution.py:99
  126.8 0.0 reduce-scatter.2.cloned.1.call-update
  126.8 0.0 all-gather.11.cloned.1.call-start
  126.9 156.1 %reduce-scatter.2.cloned.1.call-done = f32[256,3072]{0,1:T(8,128)} async-done(((f32[2048,3072]{0,1:T(8,128)}), f32[256,3072]{0,1:T(8,128)}) %reduce-scatter.2.cloned.1.call-update) | async-done | bytes 3145744 | tf_op jit(solution)/shard_map/reduce_scatter | solution.py:98
  283.0 0.0 all-gather.11.cloned.1.call-update
  283.0 0.0 copy-start.14
  283.0 3.8 fusion.6
  286.9 1.1 fusion.1
  288.0 1.6 copy.43
  289.5 14.9 %fusion = bf16[1,512,2048]{2,1,0:T(8,128)(2,1)} fusion(bf16[2048,3072]{1,0:T(8,128)(2,1)} %param.4, bf16[512,1024]{0,1:T(8,128)(2,1)} %bitcast.87, bf16[512,1024]{0,1:T(8,128)(2,1)} %bitcast.89, bf16[512,1024]{0,1:T(8,128)(2,1)} %bitcast.92), kind=kOutput, calls=%fused_computation.8 | convolution fusion | flops 6452936704 | bytes 17825792 | tf_op jit(solution)/shard_map/dot_general | solution.py:94
  304.5 198.1 %all-gather.11.cloned.1.call-done = f32[1024,3072]{0,1:T(8,128)} async-done(((f32[256,3072]{0,1:T(8,128)}), f32[1024,3072]{0,1:T(8,128)}) %all-gather.11.cloned.1.call-update) | async-done | bytes 12582928 | tf_op jit(solution)/shard_map/all_gather | solution.py:106
  502.6 15.5 %reshape.171 = f32[4,256,3072]{1,0,2:T(4,128)} reshape(f32[1024,3072]{0,1:T(8,128)} %all-gather.11.cloned.1.call-done) | data formatting | bytes 25165824 | tf_op jit(solution)/shard_map/all_gather | solution.py:106
  518.1 19.5 %reduce_sum.29 = f32[256,3072]{0,1:T(8,128)} reduce(f32[4,256,3072]{1,0,2:T(4,128)} %reshape.171, f32[]{:T(128)} %constant.7.clone.1), dimensions={0}, to_apply=%region_3.4 | reduce | flops 2359296 | bytes 15728644 | tf_op jit(solution)/shard_map/reduce_sum | solution.py:107
  537.7 3.9 broadcast_multiply_fusion
  541.6 3.5 copy.44
  (36 shorter events, 0.1 us)
Async XLA Ops:
  7.2 2.8 copy-start
  7.2 60.6 %all-gather.9.cloned.1.call-start = ((), (), s32[]{:S(2)}) async-start(), calls=%async_computation.3 | async-start | bytes 4718592 | tf_op jit(solution)/shard_map/all_gather | solution.py:46
  24.1 3.0 copy-start.3
  26.0 1.0 copy-start.6
  28.3 78.0 %all-gather.7.cloned.1.call-start = ((), (), s32[]{:S(2)}) async-start(), calls=%async_computation.2 | async-start | bytes 4718592 | tf_op jit(solution)/shard_map/all_gather | solution.py:45
  35.8 247.2 %reduce-scatter.2.cloned.1.call-start = ((), (), s32[]{:S(2)}) async-start(), calls=%async_computation.1 | async-start | bytes 28311552 | tf_op jit(solution)/shard_map/reduce_scatter | solution.py:98
  36.1 2.8 copy-start.4
  36.1 2.8 copy-start.15
  40.4 4.9 copy-start.2
  40.4 2.0 copy-start.9
  42.5 2.9 copy-start.7
  67.8 2.9 copy-start.12
  67.8 3.1 copy-start.16
  70.9 2.2 copy-start.11
  106.3 2.9 copy-start.8
  106.3 3.2 copy-start.10
  109.5 1.2 copy-start.13
  109.5 2.1 copy-start.17
  109.5 2.1 copy-start.18
  110.7 1.0 copy-start.19
  126.8 375.8 %all-gather.11.cloned.1.call-start = ((), (), s32[]{:S(2)}) async-start(), calls=%async_computation.4 | async-start | bytes 15728640 | tf_op jit(solution)/shard_map/all_gather | solution.py:106
  283.0 3.8 copy-start.5
  283.0 3.8 copy-start.14
  537.7 7.4 %copy-start.1 = (bf16[1,512,2048]{2,1,0:T(8,128)(2,1)S(1)}, bf16[1,512,2048]{2,1,0:T(8,128)(2,1)}, u32[]{:S(2)}) copy-start(bf16[1,512,2048]{2,1,0:T(8,128)(2,1)} %param.3) | copy-start | bytes 6291460
Sparse Core Ops, SparseCore 0:
  28.5 39.3 all-gather.8
  69.7 36.5 all-gather.6
  126.9 156.0 reduce-scatter.1
  284.4 218.1 all-gather.10
